TPU v7x, 32 devices: a whole 2x2x4 slice. The times are simulated.
32 devices in a mesh: grp: 4 (over z), row: 8 (over y, x, core).
Axes of the slice: x: 2, y: 2, z: 4, core: 2. Of those that a mesh axis runs over, the one named last changes fastest.
Arguments:
- theta: bfloat16 [8, 2048, 2048], P(None, ('row', 'grp')), may hold values from -6 to 6
- group_of: int32 [8], replicated, may hold values from 0 to 3, as said below
- sector_sizes: int32 [8], replicated, may hold values from 64 to 1024, as said below
- row_order: int32 [2048], P(('row', 'grp')), may hold values from 0 to 2047, as said below
- omega: bfloat16 [8, 2048, 1024], P('grp'), may hold values from -0.125 to 0.125
Outputs:
- basis: float32 [8, 2048, 1024], P('grp', 'row')
- core: float32 [2048, 8, 1024], P('row', 'grp')
Inputs may be any that keep to these rules, and one draw needn't show every extreme that they name: `group_of`: each group number is named by exactly 2 sectors. `sector_sizes`: some sector has 1024 states and some has 64. `row_order`: each aligned block of 64 entries is a permutation of that block's own row numbers.
All inputs are finite; a program needn't handle non-finite values.
Results may differ from a plain program's by a relative error of at most 0.0028.
Values may be sent and summed in bfloat16 or wider, within the bound.
A program may use at most 128 MiB of HBM per device.

v0:
```python
import jax
import jax.numpy as jnp
from jax import lax
from jax.sharding import PartitionSpec as P


def shards(theta, group_of, sector_sizes, row_order, omega):
    group_count = lax.axis_size("grp")
    group_slot = lax.axis_index("grp")
    per_group = omega.shape[0]
    width = omega.shape[2]
    left_rows = theta.shape[1]
    sorted_ids = jnp.argsort(group_of, stable=True)
    widths_all = jnp.take(sector_sizes, sorted_ids)
    widths = lax.dynamic_slice_in_dim(widths_all, group_slot * per_group, per_group)
    local_rows = row_order % left_rows
    owned = theta[sorted_ids[:, None], local_rows[None, :]]
    owned = owned.reshape(group_count, per_group, left_rows, theta.shape[2])
    arrived = lax.all_to_all(owned, "grp", split_axis=0, concat_axis=2, tiled=True)
    sector_rows = arrived[0]
    sketch = jnp.einsum("src,sck->srk", sector_rows, omega, preferred_element_type=jnp.float32)
    live_cols = lax.broadcasted_iota(jnp.int32, (per_group, 1, width), 2) < widths[:, None, None]
    sketch = jnp.where(live_cols, sketch, 0.0)
    gram_local = jnp.einsum(
        "srk,srj->skj",
        sketch,
        sketch,
        precision=lax.Precision.HIGHEST,
        preferred_element_type=jnp.float32,
    )
    gram_total = lax.psum(gram_local, "row")
    dead_diag = jnp.where(live_cols[:, 0, :], 0.0, 1.0)
    gram_total = gram_total + dead_diag[:, :, None] * jnp.eye(width, dtype=jnp.float32)[None]
    lower = jnp.linalg.cholesky(gram_total)
    basis = lax.linalg.triangular_solve(
        lower, sketch, left_side=False, lower=True, transpose_a=True
    )
    col_slice = sector_rows.astype(jnp.float32)
    core = lax.psum_scatter(
        jnp.einsum(
            "src,srk->csk",
            col_slice,
            basis,
            precision=lax.Precision.HIGHEST,
            preferred_element_type=jnp.float32,
        ),
        "row",
        scatter_dimension=0,
        tiled=True,
    )
    return (basis, core)


def solution(mesh):
    return jax.shard_map(
        shards,
        mesh=mesh,
        in_specs=(P(None, ("row", "grp"), None), P(), P(), P(("row", "grp")), P("grp", None, None)),
        out_specs=(P("grp", "row", None), P("row", "grp", None)),
        check_vma=False,
    )
```

profile of v0, /device:TPU:0, one launch (start us, length us, event | category | flops | bytes accessed | tf_op | source)
XLA Modules:
  0.0 998.5 jit_solution(6274732886168162615)
XLA Ops:
  7.2 1.8 sort.17
  11.1 11.4 %gather_fusion.1 = bf16[512,2048]{1,0:T(8,128)(2,1)} fusion(bf16[8,64,2048]{2,1,0:T(8,128)(2,1)S(1)} %copy-done, s32[512]{0:T(512)S(1)} %reshape.206), kind=kCustom, calls=%fused_computation.1 | custom fusion | bytes 4198400 | tf_op jit(solution)/shard_map/gather | solution.py:17
  22.5 6.3 all-to-all-start
  29.0 48.0 %all-to-all-done = bf16[4,2,64,2048]{3,2,1,0:T(8,128)(2,1)S(1)} async-done(((bf16[4,2,64,2048]{3,2,1,0:T(8,128)(2,1)}), bf16[4,2,64,2048]{3,2,1,0:T(8,128)(2,1)S(1)}, u32[]{:S(2)}, u32[]{:S(2)}) %all-to-all-start) | async-done | bytes 2097184 | tf_op jit(solution)/shard_map/all_to_all | solution.py:19
  77.2 6.5 convolution_select_fusion
  83.6 9.0 fusion.86
  94.3 2.5 fusion.1
  96.9 121.7 %all-reduce.3.cloned.1.call-done = f32[2,1024,1024]{1,2,0:T(8,128)} async-done(((f32[2,1024,1024]{1,2,0:T(8,128)}), f32[2,1024,1024]{1,2,0:T(8,128)}) %all-reduce.3.cloned.1.call-update) | async-done | bytes 8388624 | tf_op jit(solution)/shard_map/psum | solution.py:31
  218.6 10.3 %multiply_add_fusion = f32[2,1024,1024]{1,2,0:T(8,128)} fusion(f32[2,1024,1024]{1,2,0:T(8,128)} %all-reduce.3.cloned.1.call-done, f32[1024,1024]{0,1:T(8,128)} %fusion.1, f32[2,1024]{1,0:T(2,128)S(1)} %broadcast_select_fusion), kind=kLoop, calls=%fused_computation.7 | loop fusion | flops 4194304 | bytes 20979712 | tf_op jit(solution)/shard_map/add | solution.py:33
  228.9 8.9 copy.104
  237.8 8.4 fusion
  246.2 3.2 copy-done.2
  249.4 23.5 %custom-call.70 = f32[2,128,128]{2,1,0:T(8,128)S(1)} custom-call(f32[2,128,128]{2,1,0:T(8,128)S(1)} %cholesky.578), custom_call_target="Cholesky" | custom-call | tf_op jit(solution)/shard_map/jit(cholesky)/cholesky | solution.py:34
  272.9 19.7 %custom-call.71 = f32[2,1,128,128]{2,3,1,0:T(8,128)S(1)} custom-call(f32[2,1,128,128]{3,2,1,0:T(8,128)S(1)} %select_bitcast_fusion.6), custom_call_target="InvertDiagBlocksLowerTriangular" | custom-call | tf_op jit(solution)/shard_map/jit(cholesky)/cholesky | solution.py:34
  292.6 4.3 cholesky.253
  296.9 3.1 constant_dynamic-update-slice_fusion.32
  300.0 2.1 convolution_subtract_fusion
  303.1 23.9 %custom-call.72 = f32[2,128,128]{2,1,0:T(8,128)S(1)} custom-call(f32[2,128,128]{2,1,0:T(8,128)S(1)} %cholesky.582), custom_call_target="Cholesky" | custom-call | tf_op jit(solution)/shard_map/jit(cholesky)/cholesky | solution.py:34
  327.7 19.7 %custom-call.73 = f32[2,1,128,128]{2,3,1,0:T(8,128)S(1)} custom-call(f32[2,1,128,128]{3,2,1,0:T(8,128)S(1)} %get-tuple-element.74), custom_call_target="InvertDiagBlocksLowerTriangular" | custom-call | tf_op jit(solution)/shard_map/jit(cholesky)/cholesky | solution.py:34
  347.3 2.9 convolution_dynamic-update-slice_fusion
  350.2 3.2 fusion.12
  354.3 23.6 %custom-call.74 = f32[2,128,128]{2,1,0:T(8,128)S(1)} custom-call(f32[2,128,128]{2,1,0:T(8,128)S(1)} %cholesky.587), custom_call_target="Cholesky" | custom-call | tf_op jit(solution)/shard_map/jit(cholesky)/cholesky | solution.py:34
  378.7 19.7 %custom-call.75 = f32[2,1,128,128]{2,3,1,0:T(8,128)S(1)} custom-call(f32[2,1,128,128]{3,2,1,0:T(8,128)S(1)} %get-tuple-element.72), custom_call_target="InvertDiagBlocksLowerTriangular" | custom-call | tf_op jit(solution)/shard_map/jit(cholesky)/cholesky | solution.py:34
  398.3 2.7 convolution_dynamic-update-slice_fusion.1
  401.0 3.8 fusion.15
  405.7 23.7 %custom-call.76 = f32[2,128,128]{2,1,0:T(8,128)S(1)} custom-call(f32[2,128,128]{2,1,0:T(8,128)S(1)} %cholesky.592), custom_call_target="Cholesky" | custom-call | tf_op jit(solution)/shard_map/jit(cholesky)/cholesky | solution.py:34
  430.1 19.7 %custom-call.77 = f32[2,1,128,128]{2,3,1,0:T(8,128)S(1)} custom-call(f32[2,1,128,128]{3,2,1,0:T(8,128)S(1)} %get-tuple-element.70), custom_call_target="InvertDiagBlocksLowerTriangular" | custom-call | tf_op jit(solution)/shard_map/jit(cholesky)/cholesky | solution.py:34
  449.7 2.5 convolution_dynamic-update-slice_fusion.2
  452.2 3.8 fusion.18
  456.8 23.5 %custom-call.78 = f32[2,128,128]{2,1,0:T(8,128)S(1)} custom-call(f32[2,128,128]{2,1,0:T(8,128)S(1)} %cholesky.597), custom_call_target="Cholesky" | custom-call | tf_op jit(solution)/shard_map/jit(cholesky)/cholesky | solution.py:34
  481.0 20.1 %custom-call.79 = f32[2,1,128,128]{2,3,1,0:T(8,128)S(1)} custom-call(f32[2,1,128,128]{3,2,1,0:T(8,128)S(1)} %get-tuple-element.68), custom_call_target="InvertDiagBlocksLowerTriangular" | custom-call | tf_op jit(solution)/shard_map/jit(cholesky)/cholesky | solution.py:34
  501.1 2.3 convolution_dynamic-update-slice_fusion.3
  503.3 3.6 fusion.21
  507.6 24.9 %custom-call.80 = f32[2,128,128]{2,1,0:T(8,128)} custom-call(f32[2,128,128]{2,1,0:T(8,128)} %cholesky.602), custom_call_target="Cholesky" | custom-call | tf_op jit(solution)/shard_map/jit(cholesky)/cholesky | solution.py:34
  534.2 21.3 %custom-call.81 = f32[2,1,128,128]{2,3,1,0:T(8,128)} custom-call(f32[2,1,128,128]{3,2,1,0:T(8,128)} %get-tuple-element.66), custom_call_target="InvertDiagBlocksLowerTriangular" | custom-call | tf_op jit(solution)/shard_map/jit(cholesky)/cholesky | solution.py:34
  555.4 2.0 convolution_dynamic-update-slice_fusion.5
  557.5 3.2 fusion.24
  561.3 24.9 %custom-call.82 = f32[2,128,128]{2,1,0:T(8,128)} custom-call(f32[2,128,128]{2,1,0:T(8,128)} %cholesky.607), custom_call_target="Cholesky" | custom-call | tf_op jit(solution)/shard_map/jit(cholesky)/cholesky | solution.py:34
  587.9 21.1 %custom-call.83 = f32[2,1,128,128]{2,3,1,0:T(8,128)} custom-call(f32[2,1,128,128]{3,2,1,0:T(8,128)} %get-tuple-element.64), custom_call_target="InvertDiagBlocksLowerTriangular" | custom-call | tf_op jit(solution)/shard_map/jit(cholesky)/cholesky | solution.py:34
  609.0 1.8 convolution_dynamic-update-slice_fusion.6
  610.8 2.5 convolution_subtract_fusion.8
  613.4 23.7 %custom-call.84 = f32[2,128,128]{2,1,0:T(8,128)S(1)} custom-call(f32[2,128,128]{2,1,0:T(8,128)S(1)} %convolution_subtract_fusion.8), custom_call_target="Cholesky" | custom-call | tf_op jit(solution)/shard_map/jit(cholesky)/cholesky | solution.py:34
  637.0 2.0 select_reduce_fusion.6
  639.7 8.8 select_select_fusion
  648.5 28.2 %while.1 = (s32[]{:T(128)}, f32[2,1024,1024]{2,1,0:T(8,128)}, s32[8,2]{0,1:T(2,128)S(1)}, f32[8,2,128,128]{3,2,0,1:T(8,128)}, s32[]{:T(128)}) while((s32[]{:T(128)}, f32[2,1024,1024]{2,1,0:T(8,128)}, s32[8,2]{0,1:T(2,128)S(1)}, f32[8,2,128,128]{3,2,0,1:T(8,128)}, s32[]{:T(128)}) %tuple.69), condition=%wide.while_cond, body=%wide.while_body.sunk | while | flops 2 | bytes 263777 | solution.py:35
  649.1 2.9 bitcast_dynamic-update-slice_fusion.2
  652.6 2.9 bitcast_dynamic-update-slice_fusion.2
  656.1 2.9 bitcast_dynamic-update-slice_fusion.2
  659.7 2.9 bitcast_dynamic-update-slice_fusion.2
  663.2 2.9 bitcast_dynamic-update-slice_fusion.2
  666.7 2.9 bitcast_dynamic-update-slice_fusion.2
  670.3 2.9 bitcast_dynamic-update-slice_fusion.2
  673.8 2.9 bitcast_dynamic-update-slice_fusion.2
  676.7 158.2 %custom-call.85 = f32[2,8,128,128]{2,3,1,0:T(8,128)S(1)} custom-call(f32[2,8,128,128]{3,2,1,0:T(8,128)} %bitcast.137), custom_call_target="InvertDiagBlocksLowerTriangular" | custom-call | tf_op jit(solution)/shard_map/triangular_solve | solution.py:35
  837.4 2.0 convolution_subtract_fusion.4
  839.9 2.5 convolution_subtract_fusion.7
  842.9 2.9 convolution_subtract_fusion.3
  846.3 3.4 convolution_subtract_fusion.6
  850.2 3.8 convolution_subtract_fusion.2
  854.8 4.5 convolution_subtract_fusion.1
  861.1 9.6 convolution_bitcast_fusion
  870.7 3.0 copy.135
  873.8 113.3 %reduce-scatter.2.cloned.1.call-done = f32[256,2,1024]{0,2,1:T(8,128)} async-done(((f32[2048,2,1024]{0,2,1:T(8,128)}), f32[256,2,1024]{0,2,1:T(8,128)}) %reduce-scatter.2.cloned.1.call-update) | async-done | bytes 2097168 | tf_op jit(solution)/shard_map/reduce_scatter | solution.py:39
  987.0 4.1 copy.136
  (99 shorter events, 27.5 us)
Async XLA Ops:
  7.2 3.9 copy-start
  22.5 54.5 %all-to-all-start = ((bf16[4,2,64,2048]{3,2,1,0:T(8,128)(2,1)}), bf16[4,2,64,2048]{3,2,1,0:T(8,128)(2,1)S(1)}, u32[]{:S(2)}, u32[]{:S(2)}) async-start(bf16[4,2,64,2048]{3,2,1,0:T(8,128)(2,1)} %bitcast.135), calls=%async_computation | async-start | bytes 4194304 | tf_op jit(solution)/shard_map/all_to_all | solution.py:19
  28.8 189.8 %all-reduce.3.cloned.1.call-start = ((), (), s32[]{:S(2)}) async-start(), calls=%async_computation.2 | async-start | bytes 16777216 | tf_op jit(solution)/shard_map/psum | solution.py:31
  77.1 6.5 copy-start.4
  92.7 894.3 %reduce-scatter.2.cloned.1.call-start = ((), (), s32[]{:S(2)}) async-start(), calls=%async_computation.3 | async-start | bytes 18874368 | tf_op jit(solution)/shard_map/reduce_scatter | solution.py:39
  246.2 3.2 copy-start.2
  272.9 24.0 %copy-start.10 = (f32[2,128,128]{2,1,0:T(8,128)}, f32[2,128,128]{2,1,0:T(8,128)S(1)}, u32[]{:S(2)}) copy-start(f32[2,128,128]{2,1,0:T(8,128)S(1)} %custom-call.70) | copy-start | bytes 393220
  302.1 0.9 copy-start.6
  326.9 26.5 %copy-start.12 = (f32[2,128,128]{2,1,0:T(8,128)}, f32[2,128,128]{2,1,0:T(8,128)S(1)}, u32[]{:S(2)}) copy-start(f32[2,128,128]{2,1,0:T(8,128)S(1)} %custom-call.72) | copy-start | bytes 393220
  353.4 0.9 copy-start.7
  377.9 26.9 %copy-start.13 = (f32[2,128,128]{2,1,0:T(8,128)}, f32[2,128,128]{2,1,0:T(8,128)S(1)}, u32[]{:S(2)}) copy-start(f32[2,128,128]{2,1,0:T(8,128)S(1)} %custom-call.74) | copy-start | bytes 393220
  404.8 0.8 copy-start.8
  429.3 26.6 %copy-start.14 = (f32[2,128,128]{2,1,0:T(8,128)}, f32[2,128,128]{2,1,0:T(8,128)S(1)}, u32[]{:S(2)}) copy-start(f32[2,128,128]{2,1,0:T(8,128)S(1)} %custom-call.76) | copy-start | bytes 393220
  456.0 0.8 copy-start.9
  480.2 20.8 %copy-start.15 = (f32[2,128,128]{2,1,0:T(8,128)}, f32[2,128,128]{2,1,0:T(8,128)S(1)}, u32[]{:S(2)}) copy-start(f32[2,128,128]{2,1,0:T(8,128)S(1)} %custom-call.78) | copy-start | bytes 393220
  557.5 79.6 %copy-start.11 = (f32[2,128,128]{2,1,0:T(8,128)S(1)}, f32[2,128,128]{2,1,0:T(8,128)}, u32[]{:S(2)}) copy-start(f32[2,128,128]{2,1,0:T(8,128)} %copy-done.10) | copy-start | bytes 393220
  639.7 8.8 copy-start.16
  854.8 6.3 copy-start.5
  859.7 1.3 copy-start.3
  870.7 120.4 %copy-start.1 = (bf16[8,64,2048]{2,1,0:T(8,128)(2,1)S(1)}, bf16[8,64,2048]{2,1,0:T(8,128)(2,1)}, u32[]{:S(2)}) copy-start(bf16[8,64,2048]{2,1,0:T(8,128)(2,1)} %param.5) | copy-start | bytes 6291460
Sparse Core Ops, SparseCore 0:
  92.8 125.6 all-reduce.2
  870.9 116.1 reduce-scatter.1
where the time goes:
time: 1010 us; the launch traced here: 999 us
  other arithmetic  534 us (53%)
  waiting for transfers between devices  283 us (28%)
  matrix products  89.4 us (9%)
  local copies, waits for them, and re-layouts  70.9 us (7%)
  between operations  15 us (1%)
    another operation x30, other arithmetic, shards(): lower = jnp.linalg.cholesky(gram_total)  342 us
    another operation x4, other arithmetic, shards(): lax.linalg.triangular_solve(lower, sketch, left_side=False, lower=True, t...  168 us
    psum x1, waiting for transfers between devices, shards(): gram_total = lax.psum(gram_local, 'row')  122 us
    reduce_scatter x1, waiting for transfers between devices, shards(): lax.psum_scatter(jnp.einsum('src,srk->csk', col_slice, basis, precision=l...  113 us
    all_to_all x1, waiting for transfers between devices, shards(): lax.all_to_all(owned, 'grp', split_axis=0, concat_axis=2, tiled=True)  48 us
    another operation x14, matrix products, shards(): lower = jnp.linalg.cholesky(gram_total)  39.5 us
    another operation x24, local copies, waits for them, and re-layouts  28.2 us
    another operation x15, matrix products, shards(): lax.linalg.triangular_solve(lower, sketch, left_side=False, lower=True, t...  24.7 us
  transfers between devices with their start and end apart: 3, of which 3 were waited for; matrix products, arithmetic and copies ran while one was open for 1% of the time, Pallas kernels for 0%

commit v1 on v0

v1 whole, which is shorter than its diff:
```python
import jax
import jax.numpy as jnp
from jax import lax
from jax.experimental import pallas as pl
from jax.experimental.pallas import tpu as pltpu
from jax.sharding import PartitionSpec as P

BLK = 128
HI = lax.Precision.HIGHEST


def factor_tile(tiles):
    sub = lax.broadcasted_iota(jnp.int32, (8, BLK), 0)
    lane = lax.broadcasted_iota(jnp.int32, (8, BLK), 1)
    count = BLK // 8
    rows = [[t[8 * i:8 * i + 8, :] for i in range(count)] for t in tiles]
    for k in range(count):
        first = 8 * k
        in_block = (lane >= first) & (lane < first + 8)
        unit = jnp.where(lane == sub + first, 1.0, 0.0)
        for x in rows:
            block = x[k]
            cols = [jnp.broadcast_to(block[:, first + t:first + t + 1], (8, BLK)) for t in range(8)]
            forward = jnp.where(in_block, unit, block)
            jordan = forward
            inv = jnp.zeros((8, BLK), jnp.float32)
            piv = jnp.ones((8, BLK), jnp.float32)
            for j in range(8):
                d = jnp.broadcast_to(cols[j][j:j + 1, :], (8, BLK))
                r = 1.0 / d
                mult = jnp.where(sub == j, 0.0, cols[j] * r)
                for t in range(j + 1, 8):
                    cols[t] = cols[t] - mult * jnp.broadcast_to(cols[t][j:j + 1, :], (8, BLK))
                lead = jnp.broadcast_to(jordan[j:j + 1, :], (8, BLK))
                jordan = jordan - mult * lead
                if j < 7:
                    forward = forward - jnp.where(sub > j, mult, 0.0) * lead
                inv = jnp.where(sub == j, r, inv)
                piv = jnp.where(sub == j, d, piv)
            x[k] = forward * lax.rsqrt(piv)
            if k + 1 < count:
                z = jordan * inv
                zrow = [jnp.broadcast_to(z[t:t + 1, :], (8, BLK)) for t in range(8)]
                for i in range(k + 1, count):
                    held = x[i]
                    terms = [jnp.broadcast_to(held[:, first + t:first + t + 1], (8, BLK)) * zrow[t] for t in range(8)]
                    total = ((terms[0] + terms[1]) + (terms[2] + terms[3])) + ((terms[4] + terms[5]) + (terms[6] + terms[7]))
                    x[i] = jnp.where(in_block, 0.0, held) - total
    return [jnp.concatenate(x, axis=0) for x in rows]


def inverse_factor_kernel(gram_ref, out_ref):
    sectors, width, _ = out_ref.shape
    steps = width // BLK
    out_ref[...] = gram_ref[...]
    tri = lax.broadcasted_iota(jnp.int32, (BLK, BLK), 0) >= lax.broadcasted_iota(jnp.int32, (BLK, BLK), 1)
    row_at = lax.broadcasted_iota(jnp.int32, (BLK, width), 0)
    col_at = lax.broadcasted_iota(jnp.int32, (BLK, width), 1)

    def step(b, _):
        at = pl.multiple_of(b * BLK, BLK)
        here = pl.ds(at, BLK)
        done = factor_tile([out_ref[s, here, here] for s in range(sectors)])
        in_block = (col_at >= at) & (col_at < at + BLK)
        for s in range(sectors):
            low = jnp.where(tri, done[s], 0.0)
            panel = jnp.where(in_block, jnp.where(col_at == row_at + at, 1.0, 0.0), out_ref[s, here, :])
            out_ref[s, here, :] = jnp.dot(low, panel, precision=HI, preferred_element_type=jnp.float32)

        def trailing(i, _):
            below = pl.ds(pl.multiple_of(i * BLK, BLK), BLK)
            for s in range(sectors):
                left = out_ref[s, here, below]
                prod = lax.dot_general(left, out_ref[s, here, :], (((0,), (0,)), ((), ())), precision=HI, preferred_element_type=jnp.float32)
                out_ref[s, below, :] = jnp.where(in_block, 0.0, out_ref[s, below, :]) - prod
            return 0

        lax.fori_loop(b + 1, steps, trailing, 0)
        return 0

    lax.fori_loop(0, steps, step, 0)
    full = lax.broadcasted_iota(jnp.int32, (BLK, width), 1)
    for b in range(steps):
        for s in range(sectors):
            held = out_ref[s, b * BLK:(b + 1) * BLK, :]
            out_ref[s, b * BLK:(b + 1) * BLK, :] = jnp.where(full <= row_at + b * BLK, held, 0.0)


def inverse_factor(gram):
    sectors, width, _ = gram.shape
    return pl.pallas_call(
        inverse_factor_kernel,
        out_shape=jax.ShapeDtypeStruct(gram.shape, jnp.float32),
        in_specs=[pl.BlockSpec(memory_space=pltpu.VMEM)],
        out_specs=pl.BlockSpec(memory_space=pltpu.VMEM),
        compiler_params=pltpu.CompilerParams(vmem_limit_bytes=40 * 1024 * 1024),
        cost_estimate=pl.CostEstimate(flops=100_000_000_000, bytes_accessed=8 * gram.size, transcendentals=0),
        name="inverse_factor",
    )(gram)


def shards(theta, group_of, sector_sizes, row_order, omega):
    group_count = lax.axis_size("grp")
    group_slot = lax.axis_index("grp")
    per_group, cols, width = omega.shape
    sector_count, left_rows, _ = theta.shape
    sorted_ids = jnp.argsort(group_of, stable=True)
    widths_all = jnp.take(sector_sizes, sorted_ids)
    widths = lax.dynamic_slice_in_dim(widths_all, group_slot * per_group, per_group)
    local_rows = row_order % left_rows
    wanted = (sorted_ids[:, None] * left_rows + local_rows[None, :]).reshape(-1)
    pick = (wanted[:, None] == jnp.arange(sector_count * left_rows)[None, :]).astype(jnp.bfloat16)
    owned = jnp.dot(pick, theta.reshape(-1, cols), preferred_element_type=jnp.float32).astype(jnp.bfloat16)
    owned = owned.reshape(group_count, per_group, left_rows, cols)
    arrived = lax.all_to_all(owned, "grp", split_axis=0, concat_axis=2, tiled=True)
    sector_rows = arrived[0]
    sketch = jnp.einsum("src,sck->srk", sector_rows, omega, preferred_element_type=jnp.float32)
    live_cols = lax.broadcasted_iota(jnp.int32, (per_group, 1, width), 2) < widths[:, None, None]
    sketch = jnp.where(live_cols, sketch, 0.0)
    gram_local = jnp.einsum("srk,srj->skj", sketch, sketch, precision=HI, preferred_element_type=jnp.float32)
    gram_total = lax.psum(gram_local, "row")
    dead_diag = jnp.where(live_cols[:, 0, :], 0.0, 1.0)
    gram_total = gram_total + dead_diag[:, :, None] * jnp.eye(width, dtype=jnp.float32)[None]
    cross = jnp.einsum("src,srk->sck", sector_rows.astype(jnp.float32), sketch, precision=HI, preferred_element_type=jnp.float32)
    cross = lax.psum_scatter(cross, "row", scatter_dimension=1, tiled=True)
    inverse = inverse_factor(gram_total)
    basis = jnp.einsum("srk,sjk->srj", sketch, inverse, precision=HI, preferred_element_type=jnp.float32)
    core = jnp.einsum("sck,sjk->csj", cross, inverse, precision=HI, preferred_element_type=jnp.float32)
    return (basis, core)


def solution(mesh):
    return jax.shard_map(
        shards,
        mesh=mesh,
        in_specs=(P(None, ("row", "grp"), None), P(), P(), P(("row", "grp")), P("grp", None, None)),
        out_specs=(P("grp", "row", None), P("row", "grp", None)),
        check_vma=False,
    )
```

time: 1010 us -> 353 us (0.35); the launches traced: 999 us -> 353 us
  other arithmetic: 534 us -> 13.2 us
  waiting for transfers between devices: 283 us -> 161 us
  Pallas kernels: 0 us -> 99 us
  local copies, waits for them, and re-layouts: 70.9 us -> 8.97 us
  matrix products: 89.4 us -> 50.5 us
    another operation x34 -> x0, other arithmetic: 510 us -> none  [the longest x30 342 us: shards(): lower = jnp.linalg.cholesky(gram_total)]
    reduce_scatter x1, waiting for transfers between devices: 113 us -> 1.6 us  [shards(): cross = lax.psum_scatter(cross, 'row', scatter_dimension=1, tiled=True)]
    pallas_call x0 -> x1, Pallas kernels: none -> 99 us  [inverse_factor(): pl.pallas_call(inverse_factor_kernel, out_shape=jax.ShapeDtypeStruct(gram...]
    another operation x29 -> x0, matrix products: 64.2 us -> none  [the longest x14 39.5 us: shards(): lower = jnp.linalg.cholesky(gram_total)]
    another operation x33 -> x0, local copies, waits for them, and re-layouts: 33.8 us -> none
    dot_general x2 -> x5, matrix products: 18.7 us -> 44 us  [the longest x1 12 us: shards(): jnp.einsum('src,srk->sck', sector_rows.astype(jnp.float32), sketch, preci...]
    gather x1 -> x0, local copies, waits for them, and re-layouts: 11.4 us -> none  [shards(): owned = theta[sorted_ids[:, None], local_rows[None, :]]]
    psum x1, waiting for transfers between devices: 122 us -> 111 us  [shards(): gram_total = lax.psum(gram_local, 'row')]
  transfers between devices with their start and end apart: 3 -> 3, of which waited for: 3 -> 3; matrix products, arithmetic and copies ran while one was open for 1% -> 9% of each run, Pallas kernels for 0% -> 28%
where the time goes in v1:
time: 353 us
  waiting for transfers between devices  161 us (46%)
  Pallas kernels  99 us (28%)
  matrix products  50.5 us (14%)
  between operations  14.1 us (4%)
  other arithmetic  13.2 us (4%)
  local copies, waits for them, and re-layouts  8.97 us (3%)
  starting transfers between devices  6.54 us (2%)
    psum x1, waiting for transfers between devices, shards(): gram_total = lax.psum(gram_local, 'row')  111 us
    pallas_call x1, Pallas kernels, inverse_factor(): pl.pallas_call(inverse_factor_kernel, out_shape=jax.ShapeDtypeStruct(gram...  99 us
    all_to_all x1, waiting for transfers between devices, shards(): lax.all_to_all(owned, 'grp', split_axis=0, concat_axis=2, tiled=True)  48 us
    dot_general x1, matrix products, shards(): jnp.einsum('src,srk->sck', sector_rows.astype(jnp.float32), sketch, preci...  12 us
    dot_general x1, matrix products, shards(): jnp.einsum('sck,sjk->csj', cross, inverse, precision=HI, preferred_elemen...  11.9 us
    dot_general x1, matrix products, shards(): jnp.einsum('srk,srj->skj', sketch, sketch, precision=HI, preferred_elemen...  8.96 us
    dot_general x1, matrix products, shards(): jnp.einsum('srk,sjk->srj', sketch, inverse, precision=HI, preferred_eleme...  8.53 us
    add x1, other arithmetic, shards(): gram_total + dead_diag[:, :, None] * jnp.eye(width, dtype=jnp.float32)[None]  7.93 us
  transfers between devices with their start and end apart: 3, of which 3 were waited for; matrix products, arithmetic and copies ran while one was open for 9% of the time, Pallas kernels for 28%

profile of v1, /device:TPU:0, one launch (start us, length us, event | category | flops | bytes accessed | tf_op | source)
XLA Modules:
  0.0 352.8 jit_solution(752473384320145489)
XLA Ops:
  7.2 0.0 copy-start
  7.2 1.8 sort.17
  9.0 1.3 gather_fusion
  10.3 0.7 and_select_fusion
  10.9 0.1 broadcast_add_fusion
  11.0 0.1 add.46
  11.1 0.0 copy-done
  11.1 2.6 convolution_convert_fusion
  13.7 6.3 %all-to-all-start = ((bf16[4,2,64,2048]{3,2,1,0:T(8,128)(2,1)}), bf16[4,2,64,2048]{3,2,1,0:T(8,128)(2,1)S(1)}, u32[]{:S(2)}, u32[]{:S(2)}) async-start(bf16[4,2,64,2048]{3,2,1,0:T(8,128)(2,1)} %bitcast.19), calls=%async_computation | async-start | bytes 4194304 | tf_op jit(solution)/shard_map/all_to_all | solution.py:115
  20.0 0.0 all-reduce.2.cloned.1.call-start
  20.0 0.1 dynamic_slice.3
  20.1 0.1 iota_compare_fusion.3
  20.2 48.0 %all-to-all-done = bf16[4,2,64,2048]{3,2,1,0:T(8,128)(2,1)S(1)} async-done(((bf16[4,2,64,2048]{3,2,1,0:T(8,128)(2,1)}), bf16[4,2,64,2048]{3,2,1,0:T(8,128)(2,1)S(1)}, u32[]{:S(2)}, u32[]{:S(2)}) %all-to-all-start) | async-done | bytes 2097184 | tf_op jit(solution)/shard_map/all_to_all | solution.py:115
  68.2 0.1 copy.10
  68.4 0.0 copy-start.3
  68.4 6.5 %fusion.18 = f32[2,256,1024]{2,1,0:T(8,128)S(1)} fusion(bf16[2,256,2048]{2,1,0:T(8,128)(2,1)S(1)} %bitcast.16, bf16[2,2048,1024]{2,1,0:T(8,128)(2,1)} %param.9), kind=kOutput, calls=%fused_computation.34 | convolution fusion | flops 2147483648 | bytes 12582912 | tf_op jit(solution)/shard_map/src,sck->srk/dot_general | solution.py:117
  74.9 0.0 copy-done.3
  74.9 9.0 %fusion.5 = f32[2,1024,1024]{2,1,0:T(8,128)} fusion(f32[2,256,1024]{2,1,0:T(8,128)S(1)} %fusion.18, pred[2,1024]{1,0:T(4,128)(4,1)S(1)} %iota_compare_fusion.3), kind=kOutput, calls=%fused_computation.9 | convolution fusion | flops 6442975232 | bytes 10487808 | tf_op jit(solution)/shard_map/srk,srj->skj/dot_general | solution.py:120
  83.8 0.0 all-reduce.2.cloned.1.call-update
  83.8 0.2 reduce-scatter.2.cloned.1.call-start
  84.1 12.0 %fusion.1 = f32[2,2048,1024]{2,1,0:T(8,128)} fusion(bf16[2,256,2048]{2,1,0:T(8,128)(2,1)} %bitcast.17, f32[2,256,1024]{2,1,0:T(8,128)S(1)} %fusion.18, pred[2,1024]{1,0:T(4,128)(4,1)S(1)} %iota_compare_fusion.3), kind=kOutput, calls=%fused_computation.5 | convolution fusion | flops 12885426176 | bytes 20973568 | tf_op jit(solution)/shard_map/src,srk->sck/dot_general | solution.py:124
  96.1 0.0 reduce-scatter.2.cloned.1.call-update
  96.1 2.6 fusion
  98.7 0.1 broadcast_select_fusion
  98.7 110.9 %all-reduce.2.cloned.1.call-done = f32[2,1024,1024]{2,1,0:T(8,128)} async-done(((f32[2,1024,1024]{2,1,0:T(8,128)}), f32[2,1024,1024]{2,1,0:T(8,128)}) %all-reduce.2.cloned.1.call-update) | async-done | bytes 8388624 | tf_op jit(solution)/shard_map/psum | solution.py:121
  209.7 7.9 %multiply_add_fusion.gram_ref = f32[2,1024,1024]{2,1,0:T(8,128)} fusion(f32[2,1024,1024]{2,1,0:T(8,128)} %all-reduce.2.cloned.1.call-done, f32[1024,1024]{1,0:T(8,128)} %fusion, f32[2,1024]{1,0:T(2,128)S(1)} %broadcast_select_fusion), kind=kLoop, calls=%fused_computation.1 | loop fusion | flops 4194304 | bytes 20979712 | tf_op jit(solution)/shard_map/add | solution.py:123
  217.6 99.0 %inverse_factor.1 = f32[2,1024,1024]{2,1,0:T(8,128)S(1)} custom-call(f32[2,1024,1024]{2,1,0:T(8,128)} %multiply_add_fusion.gram_ref), custom_call_target="tpu_custom_call" | custom-call | flops 99999997952 | bytes 16777216 | tf_op jit(solution)/shard_map/inverse_factor/pallas_call | solution.py:91
  316.6 0.0 copy-start.2
  316.6 3.2 copy-done.2
  319.8 8.5 %fusion.3 = f32[2,256,1024]{2,1,0:T(8,128)} fusion(f32[2,1024,1024]{2,1,0:T(8,128)S(1)} %inverse_factor.1, f32[2,256,1024]{2,1,0:T(8,128)S(1)} %fusion.18, pred[2,1024]{1,0:T(4,128)(4,1)S(1)} %iota_compare_fusion.3), kind=kOutput, calls=%fused_computation.7 | convolution fusion | flops 6442975232 | bytes 12584960 | tf_op jit(solution)/shard_map/srk,sjk->srj/dot_general | solution.py:127
  328.3 1.6 reduce-scatter.2.cloned.1.call-done
  329.9 0.0 copy-start.1
  329.9 11.9 %convolution_bitcast_fusion = f32[256,2,1024]{0,2,1:T(8,128)} fusion(f32[2,1024,1024]{2,1,0:T(8,128)} %copy-done.2, f32[2,256,1024]{2,1,0:T(8,128)} %reduce-scatter.2.cloned.1.call-done), kind=kOutput, calls=%fused_computation.11 | convolution fusion | flops 6442450944 | bytes 12582912 | tf_op jit(solution)/shard_map/sck,sjk->csj/dot_general | solution.py:128
  341.8 4.1 %copy.12 = f32[256,2,1024]{2,1,0:T(2,128)} copy(f32[256,2,1024]{0,2,1:T(8,128)} %convolution_bitcast_fusion) | data formatting | bytes 4194304
  345.9 0.0 copy-done.1
  (4 shorter events, 0.0 us)
Async XLA Ops:
  7.2 3.9 %copy-start = (bf16[8,64,2048]{2,1,0:T(8,128)(2,1)S(1)}, bf16[8,64,2048]{2,1,0:T(8,128)(2,1)}, u32[]{:S(2)}) copy-start(bf16[8,64,2048]{2,1,0:T(8,128)(2,1)} %param.5) | copy-start | bytes 6291460
  13.7 54.5 %all-to-all-start = ((bf16[4,2,64,2048]{3,2,1,0:T(8,128)(2,1)}), bf16[4,2,64,2048]{3,2,1,0:T(8,128)(2,1)S(1)}, u32[]{:S(2)}, u32[]{:S(2)}) async-start(bf16[4,2,64,2048]{3,2,1,0:T(8,128)(2,1)} %bitcast.19), calls=%async_computation | async-start | bytes 4194304 | tf_op jit(solution)/shard_map/all_to_all | solution.py:115
  20.0 189.6 %all-reduce.2.cloned.1.call-start = ((), (), s32[]{:S(2)}) async-start(), calls=%async_computation.2 | async-start | bytes 16777216 | tf_op jit(solution)/shard_map/psum | solution.py:121
  68.4 6.5 %copy-start.3 = (bf16[1,2,4,64,2048]{4,3,2,1,0:T(8,128)(2,1)}, bf16[1,2,4,64,2048]{4,3,2,1,0:T(8,128)(2,1)S(1)}, u32[]{:S(2)}) copy-start(bf16[1,2,4,64,2048]{4,3,2,1,0:T(8,128)(2,1)S(1)} %copy.10) | copy-start | bytes 6291460
  83.8 246.1 %reduce-scatter.2.cloned.1.call-start = ((), (), s32[]{:S(2)}) async-start(), calls=%async_computation.3 | async-start | bytes 18874368 | tf_op jit(solution)/shard_map/reduce_scatter | solution.py:125
  316.6 3.2 copy-start.2
  329.9 16.0 %copy-start.1 = (bf16[8,64,2048]{2,1,0:T(8,128)(2,1)S(1)}, bf16[8,64,2048]{2,1,0:T(8,128)(2,1)}, u32[]{:S(2)}) copy-start(bf16[8,64,2048]{2,1,0:T(8,128)(2,1)} %param.5) | copy-start | bytes 6291460
Sparse Core Ops, SparseCore 0:
  84.0 125.6 all-reduce.1
  213.7 116.2 reduce-scatter.1
